TPU v7x, 32 devices: a whole 2x2x4 slice. The times are simulated.
32 devices in a mesh: mp: 8 (over z, y), dp: 4 (over x, core).
Axes of the slice: x: 2, y: 2, z: 4, core: 2. Of those that a mesh axis runs over, the one named last changes fastest.
Arguments:
- forward_fields: bfloat16 [16, 4, 16384], P(None, None, 'mp'), may hold values from -6 to 6
- adjoint_fields: bfloat16 [64, 4, 16384], P(None, None, 'mp'), may hold values from -6 to 6
- data_rec: int32 [768], P('dp'), may hold values from 0 to 63
- data_freq: int32 [768], P('dp'), may hold values from 0 to 15
- data_coef: float32 [768, 4], P('dp'), may hold values from -6 to 6
- residual_cols: bfloat16 [768, 256], P('dp'), may hold values from -6 to 6
Outputs:
- data_update: bfloat16 [768, 256], P('dp')
- model_update: float32 [16384, 256], P(('mp', 'dp'))
All inputs are finite; a program needn't handle non-finite values.
Results may differ from a plain program's by a relative error of at most 0.0075.
Values may be sent and summed in bfloat16 or wider, within the bound.
A program may use at most 64 MiB of HBM per device.

v0:
```python
import math
import jax
import jax.numpy as jnp
from jax import lax
from jax.sharding import PartitionSpec as P

GRID_COLS = 128
SWEEPS = 2


def with_halo(array, sides, width):
    for axis, dim in sides:
        peers, length = (lax.axis_size(axis), array.shape[dim])
        up = [(i, (i + 1) % peers) for i in range(peers - 1)]
        down = [(j, i) for i, j in up]
        last = lax.slice_in_dim(array, length - width, length, axis=dim)
        leading = lax.slice_in_dim(array, 0, width, axis=dim)
        before = lax.ppermute(last, axis, up)
        after = lax.ppermute(leading, axis, down)
        array = jnp.concatenate([before, array, after], axis=dim)
    return array


def sweep_once(field):
    center = field[:, 1:-1, :]
    sides = jnp.pad(center, ((0, 0), (0, 0), (1, 1)))
    beside_all = field[:, :-2, :] + field[:, 2:, :] + sides[:, :, :-2] + sides[:, :, 2:]
    return center + 0.2 * (beside_all - 4.0 * center)


def per_device(forward_fields, adjoint_fields, data_rec, data_freq, data_coef, residual_cols):
    rows_here = data_rec.shape[0]
    cells_here = forward_fields.shape[2]
    slab_rows = cells_here // GRID_COLS
    slab_count = lax.axis_size("mp")
    block_count = lax.axis_size("dp")
    adjoint = adjoint_fields[data_rec].astype(jnp.float32)
    forward = forward_fields[data_freq].astype(jnp.float32)
    sens = (0.5 * jnp.sum(data_coef[:, :, None] * adjoint * forward, axis=1)).astype(jnp.bfloat16)
    grid = sens.astype(jnp.float32).reshape(rows_here, slab_rows, GRID_COLS)
    extended = with_halo(grid.astype(jnp.bfloat16), (("mp", 1),), SWEEPS).astype(grid.dtype)
    first_row = lax.axis_index("mp") * slab_rows
    total_rows = slab_rows * slab_count
    for sweep in range(SWEEPS):
        extended = sweep_once(extended)
        margin = SWEEPS - 1 - sweep
        if margin > 0:
            global_rows = first_row - margin + jnp.arange(slab_rows + 2 * margin, dtype=jnp.int32)
            inside = (global_rows >= 0) & (global_rows < total_rows)
            extended = jnp.where(inside[None, :, None], extended, 0.0)
    grid = extended
    smooth = grid.reshape(rows_here, cells_here).astype(jnp.bfloat16)
    residual_whole = lax.all_gather(residual_cols, "dp", axis=0, tiled=True)
    gram_tile = lax.dot_general(
        smooth,
        lax.all_gather(sens, "dp", axis=0, tiled=True),
        (((1,), (1,)), ((), ())),
        preferred_element_type=jnp.float32,
    )
    partial_value = jnp.dot(
        gram_tile, residual_whole.astype(jnp.float32), precision=lax.Precision.HIGHEST
    )
    gram_prod = lax.psum(partial_value, "mp") / (cells_here * slab_count)
    data_update = (gram_prod + residual_cols.astype(jnp.float32)).astype(jnp.bfloat16)
    summed = lax.psum_scatter(
        lax.dot_general(
            smooth, data_update, (((0,), (0,)), ((), ())), preferred_element_type=jnp.float32
        ),
        "dp",
        scatter_dimension=0,
        tiled=True,
    )
    model_update = summed / math.sqrt(rows_here * block_count)
    return (data_update, model_update)


def solution(mesh):
    in_specs = (
        P(None, None, "mp"),
        P(None, None, "mp"),
        P("dp"),
        P("dp"),
        P("dp", None),
        P("dp", None),
    )
    out_specs = (P("dp", None), P(("mp", "dp"), None))
    return jax.shard_map(
        per_device, mesh=mesh, in_specs=in_specs, out_specs=out_specs, check_vma=False
    )
```

profile of v0, /device:TPU:0, one launch (start us, length us, event | category | flops | bytes accessed | tf_op | source)
XLA Modules:
  0.0 189.3 jit_solution(5085543405692865950)
XLA Ops:
  7.2 0.0 copy-start
  7.2 0.0 all-gather.2.cloned.1.call-start
  7.2 0.8 compare_select_fusion.1
  8.0 0.7 compare_select_fusion
  8.7 0.8 copy.10
  9.5 9.6 %gather_fusion = bf16[192,4,2048]{2,1,0:T(4,128)(2,1)} fusion(bf16[64,4,2048]{2,1,0:T(4,128)(2,1)S(1)} %copy-done, s32[1024]{0:T(1024)S(1)} %pad_clamp_fusion.1), kind=kCustom, calls=%fused_computation | custom fusion | bytes 6292224 | tf_op jit(solution)/shard_map/gather | solution.py:37
  19.1 9.7 %gather_fusion.1 = bf16[192,4,2048]{2,1,0:T(4,128)(2,1)} fusion(bf16[16,4,2048]{2,1,0:T(4,128)(2,1)S(1)} %copy-done.1, s32[1024]{0:T(1024)S(1)} %pad_clamp_fusion), kind=kCustom, calls=%fused_computation.1 | custom fusion | bytes 6292224 | tf_op jit(solution)/shard_map/gather | solution.py:38
  28.8 9.7 %multiply_reduce_fusion = f32[192,2048]{1,0:T(8,128)S(1)} fusion(bf16[192,4,2048]{2,1,0:T(4,128)(2,1)} %gather_fusion.1, bf16[192,4,2048]{2,1,0:T(4,128)(2,1)} %gather_fusion, f32[192,4]{1,0:T(8,128)S(1)} %copy.10), kind=kLoop, calls=%fused_computation.2 | loop fusion | flops 7471104 | bytes 7867392 | tf_op jit(solution)/shard_map/reduce_sum | solution.py:39
  38.5 1.0 multiply_convert_fusion
  39.5 0.0 all-gather.2.cloned.1.call-update
  39.5 0.0 all-reduce.4.cloned.1.call-start
  39.6 1.4 copy.14
  41.0 4.9 %collective-permute-start = (bf16[192,2,128]{0,2,1:T(8,128)(2,1)S(1)}, bf16[192,2,128]{0,2,1:T(8,128)(2,1)S(1)}, u32[]{:S(2)}, u32[]{:S(2)}) collective-permute-start(bf16[192,2,128]{0,2,1:T(8,128)(2,1)S(1)} %get-tuple-element.2), channel_id=1, source_target_pairs={{0,4},{4,8},{8,12},{12,16},{16,20},{20,24},{24,28},{1,5},{5,9},{9,... | collective-permute-start | bytes 294920 | tf_op jit(solution)/shard_map/ppermute | solution.py:18
  46.0 1.3 collective-permute-start.1
  47.3 7.1 %all_gather.7 = bf16[768,256]{1,0:T(8,128)(2,1)S(1)} all-gather(bf16[192,256]{1,0:T(8,128)(2,1)S(1)} %copy-done.3), channel_id=1, replica_groups=mesh['mp'=8,'dp'=4] {'dp'}, dimensions={0}, use_global_device_ids=true | all-gather | bytes 491520 | tf_op jit(solution)/shard_map/all_gather | solution.py:53
  54.4 0.3 maximum_convert_fusion
  54.7 0.2 slice.54
  54.9 1.0 fusion.5
  55.9 0.1 slice.57
  56.1 0.8 fusion.11
  56.9 14.4 %all-gather.2.cloned.1.call-done = bf16[768,2048]{1,0:T(8,128)(2,1)} async-done(((bf16[192,2048]{1,0:T(8,128)(2,1)}), bf16[768,2048]{1,0:T(8,128)(2,1)}) %all-gather.2.cloned.1.call-update) | async-done | bytes 3145744 | tf_op jit(solution)/shard_map/all_gather | solution.py:56
  71.3 3.1 %fusion.13 = f32[192,768]{1,0:T(8,128)S(1)} fusion(bf16[192,2048]{0,1:T(8,128)(2,1)S(1)} %bitcast.10, bf16[768,2048]{1,0:T(8,128)(2,1)} %all-gather.2.cloned.1.call-done), kind=kOutput, calls=%fused_computation.31 | convolution fusion | flops 603979776 | bytes 4521984 | tf_op jit(solution)/shard_map/dot_general | solution.py:54
  74.4 1.1 fusion.14
  75.5 0.0 all-reduce.4.cloned.1.call-update
  75.5 0.0 reduce-scatter.2.cloned.1.call-start
  75.6 72.2 %all-reduce.4.cloned.1.call-done = f32[192,256]{1,0:T(8,128)} async-done(((f32[192,256]{1,0:T(8,128)}), f32[192,256]{1,0:T(8,128)}) %all-reduce.4.cloned.1.call-update) | async-done | bytes 196624 | tf_op jit(solution)/shard_map/psum | solution.py:63
  147.8 1.0 add_convert_fusion
  148.7 0.0 copy-start.2
  148.7 1.8 fusion.15
  150.5 0.0 reduce-scatter.2.cloned.1.call-update
  150.5 30.3 %reduce-scatter.2.cloned.1.call-done = f32[512,256]{1,0:T(8,128)} async-done(((f32[2048,256]{1,0:T(8,128)}), f32[512,256]{1,0:T(8,128)}) %reduce-scatter.2.cloned.1.call-update) | async-done | bytes 524304 | tf_op jit(solution)/shard_map/reduce_scatter | solution.py:65
  180.9 1.9 broadcast_multiply_fusion
  (12 shorter events, 0.1 us)
Async XLA Ops:
  7.2 2.3 %copy-start = (bf16[64,4,2048]{2,1,0:T(4,128)(2,1)S(1)}, bf16[64,4,2048]{2,1,0:T(4,128)(2,1)}, u32[]{:S(2)}) copy-start(bf16[64,4,2048]{2,1,0:T(4,128)(2,1)} %param.7) | copy-start | bytes 3145732
  7.2 64.1 %all-gather.2.cloned.1.call-start = ((), (), s32[]{:S(2)}) async-start(), calls=%async_computation.1 | async-start | bytes 3932160 | tf_op jit(solution)/shard_map/all_gather | solution.py:56
  9.5 9.6 %copy-start.1 = (bf16[16,4,2048]{2,1,0:T(4,128)(2,1)S(1)}, bf16[16,4,2048]{2,1,0:T(4,128)(2,1)}, u32[]{:S(2)}) copy-start(bf16[16,4,2048]{2,1,0:T(4,128)(2,1)} %param.6) | copy-start | bytes 786436
  38.5 8.8 %copy-start.3 = (bf16[192,256]{1,0:T(8,128)(2,1)S(1)}, bf16[192,256]{1,0:T(8,128)(2,1)}, u32[]{:S(2)}) copy-start(bf16[192,256]{1,0:T(8,128)(2,1)} %param.11) | copy-start | bytes 294916
  39.5 108.3 %all-reduce.4.cloned.1.call-start = ((), (), s32[]{:S(2)}) async-start(), calls=%async_computation.2 | async-start | bytes 393216 | tf_op jit(solution)/shard_map/psum | solution.py:63
  41.0 13.3 %collective-permute-start = (bf16[192,2,128]{0,2,1:T(8,128)(2,1)S(1)}, bf16[192,2,128]{0,2,1:T(8,128)(2,1)S(1)}, u32[]{:S(2)}, u32[]{:S(2)}) collective-permute-start(bf16[192,2,128]{0,2,1:T(8,128)(2,1)S(1)} %get-tuple-element.2), channel_id=1, source_target_pairs={{0,4},{4,8},{8,12},{12,16},{16,20},{20,24},{24,28},{1,5},{5,9},{9,... | collective-permute-start | bytes 294920 | tf_op jit(solution)/shard_map/ppermute | solution.py:18
  46.0 8.4 %collective-permute-start.1 = (bf16[192,2,128]{0,2,1:T(8,128)(2,1)S(1)}, bf16[192,2,128]{0,2,1:T(8,128)(2,1)S(1)}, u32[]{:S(2)}, u32[]{:S(2)}) collective-permute-start(bf16[192,2,128]{0,2,1:T(8,128)(2,1)S(1)} %get-tuple-element.3), channel_id=1, source_target_pairs={{4,0},{8,4},{12,8},{16,12},{20,16},{24,20},{28,24},{5,1},{9,5},{13... | collective-permute-start | bytes 294920 | tf_op jit(solution)/shard_map/ppermute | solution.py:19
  75.5 105.4 %reduce-scatter.2.cloned.1.call-start = ((), (), s32[]{:S(2)}) async-start(), calls=%async_computation.3 | async-start | bytes 2621440 | tf_op jit(solution)/shard_map/reduce_scatter | solution.py:65
  148.7 1.8 copy-start.2
Sparse Core Ops, SparseCore 0:
  39.6 31.6 all-gather.1
  75.7 72.0 all-reduce.3
  150.7 30.1 reduce-scatter.1
where the time goes:
time: 190 us; the launch traced here: 189 us
  waiting for transfers between devices  117 us (62%)
  local copies, waits for them, and re-layouts  21.9 us (12%)
  other arithmetic  17.1 us (9%)
  between operations  13.9 us (7%)
  blocking collectives  7.1 us (4%)
  starting transfers between devices  6.32 us (3%)
  matrix products  5.98 us (3%)
    psum x1, waiting for transfers between devices, per_device(): gram_prod = lax.psum(partial_value, 'mp') / (cells_here * slab_count)  72.2 us
    reduce_scatter x1, waiting for transfers between devices, per_device(): lax.psum_scatter(lax.dot_general(smooth, data_update, (((0,), (0,)), ((),...  30.3 us
    all_gather x1, waiting for transfers between devices, per_device(): lax.all_gather(sens, 'dp', axis=0, tiled=True)  14.4 us
    gather x1, local copies, waits for them, and re-layouts, per_device(): forward = forward_fields[data_freq].astype(jnp.float32)  9.69 us
    reduce_sum x1, other arithmetic, per_device(): jnp.sum(data_coef[:, :, None] * adjoint * forward, axis=1)  9.66 us
    gather x1, local copies, waits for them, and re-layouts, per_device(): adjoint = adjoint_fields[data_rec].astype(jnp.float32)  9.62 us
    all_gather x1, blocking collectives, per_device(): residual_whole = lax.all_gather(residual_cols, 'dp', axis=0, tiled=True)  7.1 us
    ppermute x1, starting transfers between devices, with_halo(): before = lax.ppermute(last, axis, up)  4.91 us
  transfers between devices with their start and end apart: 5, of which 3 were waited for; matrix products, arithmetic and copies ran while one was open for 2% of the time, Pallas kernels for 0%

commit v1 on v0

--- a/solution.py
+++ b/solution.py
@@ -60,7 +60,7 @@
     partial_value = jnp.dot(
         gram_tile, residual_whole.astype(jnp.float32), precision=lax.Precision.HIGHEST
     )
-    gram_prod = lax.psum(partial_value, "mp") / (cells_here * slab_count)
+    gram_prod = jnp.sum(lax.all_gather(partial_value, "mp"), axis=0) / (cells_here * slab_count)
     data_update = (gram_prod + residual_cols.astype(jnp.float32)).astype(jnp.bfloat16)
     summed = lax.psum_scatter(
         lax.dot_general(

time: 190 us -> 163 us (0.86)
  waiting for transfers between devices: 117 us -> 89.8 us
    psum x1 -> x0, waiting for transfers between devices: 72.2 us -> none  [per_device(): gram_prod = lax.psum(partial_value, 'mp') / (cells_here * slab_count)]
    all_gather x0 -> x1, waiting for transfers between devices: none -> 45.7 us  [per_device(): lax.all_gather(partial_value, 'mp')]
where the time goes in v1:
time: 163 us
  waiting for transfers between devices  89.8 us (55%)
  local copies, waits for them, and re-layouts  21.9 us (13%)
  other arithmetic  17.7 us (11%)
  between operations  13.9 us (9%)
  blocking collectives  7.1 us (4%)
  starting transfers between devices  6.32 us (4%)
  matrix products  5.99 us (4%)
    all_gather x1, waiting for transfers between devices, per_device(): lax.all_gather(partial_value, 'mp')  45.7 us
    reduce_scatter x1, waiting for transfers between devices, per_device(): lax.psum_scatter(lax.dot_general(smooth, data_update, (((0,), (0,)), ((),...  29.7 us
    all_gather x1, waiting for transfers between devices, per_device(): lax.all_gather(sens, 'dp', axis=0, tiled=True)  14.4 us
    gather x1, local copies, waits for them, and re-layouts, per_device(): forward = forward_fields[data_freq].astype(jnp.float32)  9.69 us
    reduce_sum x1, other arithmetic, per_device(): jnp.sum(data_coef[:, :, None] * adjoint * forward, axis=1)  9.66 us
    gather x1, local copies, waits for them, and re-layouts, per_device(): adjoint = adjoint_fields[data_rec].astype(jnp.float32)  9.62 us
    all_gather x1, blocking collectives, per_device(): residual_whole = lax.all_gather(residual_cols, 'dp', axis=0, tiled=True)  7.1 us
    ppermute x1, starting transfers between devices, with_halo(): before = lax.ppermute(last, axis, up)  4.91 us
  transfers between devices with their start and end apart: 5, of which 3 were waited for; matrix products, arithmetic and copies ran while one was open for 2% of the time, Pallas kernels for 0%

profile of v1, /device:TPU:0, one launch (start us, length us, event | category | flops | bytes accessed | tf_op | source)
XLA Modules:
  0.0 162.8 jit_solution(4962106662269690026)
XLA Ops:
  7.2 0.0 copy-start
  7.2 0.0 all-gather.4.cloned.1.call-start
  7.2 0.8 compare_select_fusion.1
  8.0 0.7 compare_select_fusion
  8.7 0.8 copy.10
  9.5 9.6 %gather_fusion = bf16[192,4,2048]{2,1,0:T(4,128)(2,1)} fusion(bf16[64,4,2048]{2,1,0:T(4,128)(2,1)S(1)} %copy-done, s32[1024]{0:T(1024)S(1)} %pad_clamp_fusion.1), kind=kCustom, calls=%fused_computation | custom fusion | bytes 6292224 | tf_op jit(solution)/shard_map/gather | solution.py:37
  19.1 9.7 %gather_fusion.1 = bf16[192,4,2048]{2,1,0:T(4,128)(2,1)} fusion(bf16[16,4,2048]{2,1,0:T(4,128)(2,1)S(1)} %copy-done.1, s32[1024]{0:T(1024)S(1)} %pad_clamp_fusion), kind=kCustom, calls=%fused_computation.1 | custom fusion | bytes 6292224 | tf_op jit(solution)/shard_map/gather | solution.py:38
  28.8 9.7 %multiply_reduce_fusion = f32[192,2048]{1,0:T(8,128)S(1)} fusion(bf16[192,4,2048]{2,1,0:T(4,128)(2,1)} %gather_fusion.1, bf16[192,4,2048]{2,1,0:T(4,128)(2,1)} %gather_fusion, f32[192,4]{1,0:T(8,128)S(1)} %copy.10), kind=kLoop, calls=%fused_computation.2 | loop fusion | flops 7471104 | bytes 7867392 | tf_op jit(solution)/shard_map/reduce_sum | solution.py:39
  38.5 1.0 multiply_convert_fusion
  39.5 0.0 all-gather.4.cloned.1.call-update
  39.5 0.0 all-gather.6.cloned.1.call-start
  39.6 1.4 copy.14
  41.0 4.9 %collective-permute-start = (bf16[192,2,128]{0,2,1:T(8,128)(2,1)S(1)}, bf16[192,2,128]{0,2,1:T(8,128)(2,1)S(1)}, u32[]{:S(2)}, u32[]{:S(2)}) collective-permute-start(bf16[192,2,128]{0,2,1:T(8,128)(2,1)S(1)} %get-tuple-element.2), channel_id=1, source_target_pairs={{0,4},{4,8},{8,12},{12,16},{16,20},{20,24},{24,28},{1,5},{5,9},{9,... | collective-permute-start | bytes 294920 | tf_op jit(solution)/shard_map/ppermute | solution.py:18
  46.0 1.3 collective-permute-start.1
  47.3 7.1 %all_gather.13 = bf16[768,256]{1,0:T(8,128)(2,1)S(1)} all-gather(bf16[192,256]{1,0:T(8,128)(2,1)S(1)} %copy-done.3), channel_id=1, replica_groups=mesh['mp'=8,'dp'=4] {'dp'}, dimensions={0}, use_global_device_ids=true | all-gather | bytes 491520 | tf_op jit(solution)/shard_map/all_gather | solution.py:53
  54.4 0.3 maximum_convert_fusion
  54.7 0.2 slice.54
  54.9 1.0 fusion.5
  55.9 0.1 slice.57
  56.1 0.8 fusion.11
  56.9 14.4 %all-gather.4.cloned.1.call-done = bf16[768,2048]{1,0:T(8,128)(2,1)} async-done(((bf16[192,2048]{1,0:T(8,128)(2,1)}), bf16[768,2048]{1,0:T(8,128)(2,1)}) %all-gather.4.cloned.1.call-update) | async-done | bytes 3145744 | tf_op jit(solution)/shard_map/all_gather | solution.py:56
  71.3 3.1 %fusion.13 = f32[192,768]{1,0:T(8,128)S(1)} fusion(bf16[192,2048]{0,1:T(8,128)(2,1)S(1)} %bitcast.11, bf16[768,2048]{1,0:T(8,128)(2,1)} %all-gather.4.cloned.1.call-done), kind=kOutput, calls=%fused_computation.31 | convolution fusion | flops 603979776 | bytes 4521984 | tf_op jit(solution)/shard_map/dot_general | solution.py:54
  74.4 1.1 fusion.14
  75.5 0.0 all-gather.6.cloned.1.call-update
  75.5 0.0 reduce-scatter.2.cloned.1.call-start
  75.6 45.7 %all-gather.6.cloned.1.call-done = f32[1536,256]{1,0:T(8,128)} async-done(((f32[192,256]{1,0:T(8,128)}), f32[1536,256]{1,0:T(8,128)}) %all-gather.6.cloned.1.call-update) | async-done | bytes 1572880 | tf_op jit(solution)/shard_map/all_gather | solution.py:63
  121.3 1.5 reduce_sum.19
  122.9 0.0 copy-start.2
  122.9 1.8 %fusion.15 = f32[2048,256]{1,0:T(8,128)} fusion(bf16[192,2048]{0,1:T(8,128)(2,1)S(1)} %bitcast.12, bf16[192,256]{1,0:T(8,128)(2,1)S(1)} %add_convert_fusion), kind=kOutput, calls=%fused_computation.33 | convolution fusion | flops 201326592 | bytes 2981888 | tf_op jit(solution)/shard_map/dot_general | solution.py:66
  124.7 0.0 reduce-scatter.2.cloned.1.call-update
  124.7 29.7 %reduce-scatter.2.cloned.1.call-done = f32[512,256]{1,0:T(8,128)} async-done(((f32[2048,256]{1,0:T(8,128)}), f32[512,256]{1,0:T(8,128)}) %reduce-scatter.2.cloned.1.call-update) | async-done | bytes 524304 | tf_op jit(solution)/shard_map/reduce_scatter | solution.py:65
  154.4 1.9 %broadcast_multiply_fusion = f32[512,256]{1,0:T(8,128)} fusion(f32[512,256]{1,0:T(8,128)} %reduce-scatter.2.cloned.1.call-done), kind=kLoop, calls=%fused_computation.23 | loop fusion | flops 131072 | bytes 1048576 | tf_op jit(solution)/shard_map/div | solution.py:73
  (13 shorter events, 0.1 us)
Async XLA Ops:
  7.2 2.3 %copy-start = (bf16[64,4,2048]{2,1,0:T(4,128)(2,1)S(1)}, bf16[64,4,2048]{2,1,0:T(4,128)(2,1)}, u32[]{:S(2)}) copy-start(bf16[64,4,2048]{2,1,0:T(4,128)(2,1)} %param.7) | copy-start | bytes 3145732
  7.2 64.1 %all-gather.4.cloned.1.call-start = ((), (), s32[]{:S(2)}) async-start(), calls=%async_computation.1 | async-start | bytes 3932160 | tf_op jit(solution)/shard_map/all_gather | solution.py:56
  9.5 9.6 %copy-start.1 = (bf16[16,4,2048]{2,1,0:T(4,128)(2,1)S(1)}, bf16[16,4,2048]{2,1,0:T(4,128)(2,1)}, u32[]{:S(2)}) copy-start(bf16[16,4,2048]{2,1,0:T(4,128)(2,1)} %param.6) | copy-start | bytes 786436
  38.5 8.8 %copy-start.3 = (bf16[192,256]{1,0:T(8,128)(2,1)S(1)}, bf16[192,256]{1,0:T(8,128)(2,1)}, u32[]{:S(2)}) copy-start(bf16[192,256]{1,0:T(8,128)(2,1)} %param.11) | copy-start | bytes 294916
  39.5 81.8 %all-gather.6.cloned.1.call-start = ((), (), s32[]{:S(2)}) async-start(), calls=%async_computation.3 | async-start | bytes 1769472 | tf_op jit(solution)/shard_map/all_gather | solution.py:63
  41.0 13.3 %collective-permute-start = (bf16[192,2,128]{0,2,1:T(8,128)(2,1)S(1)}, bf16[192,2,128]{0,2,1:T(8,128)(2,1)S(1)}, u32[]{:S(2)}, u32[]{:S(2)}) collective-permute-start(bf16[192,2,128]{0,2,1:T(8,128)(2,1)S(1)} %get-tuple-element.2), channel_id=1, source_target_pairs={{0,4},{4,8},{8,12},{12,16},{16,20},{20,24},{24,28},{1,5},{5,9},{9,... | collective-permute-start | bytes 294920 | tf_op jit(solution)/shard_map/ppermute | solution.py:18
  46.0 8.4 %collective-permute-start.1 = (bf16[192,2,128]{0,2,1:T(8,128)(2,1)S(1)}, bf16[192,2,128]{0,2,1:T(8,128)(2,1)S(1)}, u32[]{:S(2)}, u32[]{:S(2)}) collective-permute-start(bf16[192,2,128]{0,2,1:T(8,128)(2,1)S(1)} %get-tuple-element.3), channel_id=1, source_target_pairs={{4,0},{8,4},{12,8},{16,12},{20,16},{24,20},{28,24},{5,1},{9,5},{13... | collective-permute-start | bytes 294920 | tf_op jit(solution)/shard_map/ppermute | solution.py:19
  75.5 78.8 %reduce-scatter.2.cloned.1.call-start = ((), (), s32[]{:S(2)}) async-start(), calls=%async_computation.2 | async-start | bytes 2621440 | tf_op jit(solution)/shard_map/reduce_scatter | solution.py:65
  122.9 1.8 %copy-start.2 = (bf16[192,256]{1,0:T(8,128)(2,1)}, bf16[192,256]{1,0:T(8,128)(2,1)S(1)}, u32[]{:S(2)}) copy-start(bf16[192,256]{1,0:T(8,128)(2,1)S(1)} %add_convert_fusion) | copy-start | bytes 294916
Sparse Core Ops, SparseCore 0:
  39.6 31.6 all-gather.3
  75.7 45.6 all-gather.5
  124.8 29.5 reduce-scatter.1
